TPU v7x, 32 devices: a whole 2x2x4 slice. The times are simulated.
32 devices in a mesh: seq: 16 (over z, y, x), tp: 2 (over core).
Axes of the slice: x: 2, y: 2, z: 4, core: 2. Of those that a mesh axis runs over, the one named last changes fastest.
Arguments:
- tokens: bfloat16 [2048, 2048], P('seq'), may hold values from -6 to 6
- cotangent: bfloat16 [2048, 2048], P('seq'), may hold values from -6 to 6
- block_order: int32 [32], replicated, may hold values from 0 to 31, each once
- sequence_ids: int32 [2048], replicated, may hold values from 0 to 1, never falling along the last dimension, each value on 1 to 1536 neighbouring positions
- attn_gain: float32 [2048], P('seq'), may hold values from 0.5 to 1.5
- w_query: float32 [2048, 2048], P('seq', 'tp'), may hold values from -0.125 to 0.125
- w_key: float32 [2048, 2048], P('seq', 'tp'), may hold values from -0.125 to 0.125
- w_value: float32 [2048, 2048], P('seq', 'tp'), may hold values from -0.125 to 0.125
- w_out: float32 [2048, 2048], P('tp', 'seq'), may hold values from -2 to 2
- mlp_gain: float32 [2048], P('seq'), may hold values from 0.5 to 1.5
- w_gate: float32 [2048, 8192], P('seq', 'tp'), may hold values from -0.125 to 0.125
- w_up: float32 [2048, 8192], P('seq', 'tp'), may hold values from -0.125 to 0.125
- w_down: float32 [8192, 2048], P('tp', 'seq'), may hold values from -0.0625 to 0.0625
Outputs:
- output: bfloat16 [2048, 2048], P('seq')
- grad_tokens: float32 [2048, 2048], P('seq')
- grad_attn_gain: float32 [2048], P('seq')
- grad_query: float32 [2048, 2048], P('seq', 'tp')
- grad_key: float32 [2048, 2048], P('seq', 'tp')
- grad_value: float32 [2048, 2048], P('seq', 'tp')
- grad_out: float32 [2048, 2048], P('tp', 'seq')
- grad_mlp_gain: float32 [2048], P('seq')
- grad_gate: float32 [2048, 8192], P('seq', 'tp')
- grad_up: float32 [2048, 8192], P('seq', 'tp')
- grad_down: float32 [8192, 2048], P('tp', 'seq')
Inputs may be any that keep to these rules, and one draw needn't show every extreme that they name: `block_order`: each block number appears once. `sequence_ids`: never falls along the positions; the first sequence has from 512 to 1536 tokens and the second the rest.
All inputs are finite; a program needn't handle non-finite values.
Results may differ from a plain program's by a relative error of at most 0.015.
Values may be sent and summed in bfloat16 or wider, within the bound.
A program may use at most 256 MiB of HBM per device.

v0:
```python
import math

import jax
import jax.numpy as jnp
from jax import lax
from jax.sharding import PartitionSpec as P

HD = 128


EPS = 1e-05
ROPE_BASE = 10000.0


def from_behind(value, axis, by):
    length = lax.axis_size(axis)
    return lax.ppermute(value, axis, [(i, (i + by) % length) for i in range(length)])


def group_positions(block_order, start, count, group_rows):
    row_ids = start + jnp.arange(count, dtype=jnp.int32)
    which = row_ids // group_rows
    slots = jnp.arange(block_order.shape[0], dtype=jnp.int32)
    onehot = (which[:, None] == slots[None, :]).astype(jnp.int32)
    first_pos = jnp.sum(onehot * block_order[None, :], axis=1)
    return first_pos * group_rows + row_ids % group_rows


def visible(query_pos, key_pos, boundary):
    query_seg = query_pos >= boundary
    key_seg = key_pos >= boundary
    return (key_pos[None, :] <= query_pos[:, None]) & (key_seg[None, :] == query_seg[:, None])


def normalize(values):
    inverse = lax.rsqrt(jnp.mean(values * values, axis=-1, keepdims=True) + EPS)
    return (values * inverse, inverse)


def norm_back(grad_normed, normed, inverse):
    return inverse * (grad_normed - normed * jnp.mean(grad_normed * normed, axis=-1, keepdims=True))


def rope_tables(positions, head_dim):
    half_dim = head_dim // 2
    freqs = ROPE_BASE ** (-(jnp.arange(half_dim, dtype=jnp.float32) * 2.0 / head_dim))
    angles = positions.astype(jnp.float32)[:, None] * freqs[None, :]
    return (jnp.cos(angles), jnp.sin(angles))


def rotate(field_in, cosine, sine):
    half_dim = field_in.shape[-1] // 2
    first_half = field_in[..., :half_dim]
    second_half = field_in[..., half_dim:]
    cos_part = cosine[:, None, :]
    sin_part = sine[:, None, :]
    return jnp.concatenate(
        [
            first_half * cos_part - second_half * sin_part,
            second_half * cos_part + first_half * sin_part,
        ],
        axis=-1,
    )


def unrotate(field_in, cosine, sine):
    half_dim = field_in.shape[-1] // 2
    first_half = field_in[..., :half_dim]
    second_half = field_in[..., half_dim:]
    cos_part = cosine[:, None, :]
    sin_part = sine[:, None, :]
    return jnp.concatenate(
        [
            first_half * cos_part + second_half * sin_part,
            second_half * cos_part - first_half * sin_part,
        ],
        axis=-1,
    )


def pair_terms(
    query_blk,
    gradout_blk,
    query_pos,
    key_blk,
    value_blk,
    key_pos,
    boundary,
    score_scale,
    score_bias,
):
    allowed = visible(query_pos, key_pos, boundary)

    def pair_compute(unused):
        scores = (
            jnp.einsum("qhd,khd->hqk", query_blk, key_blk, preferred_element_type=jnp.float32)
            * score_scale
            + score_bias
        )
        sigmas = jax.nn.sigmoid(scores)
        weights = jnp.where(allowed[None], sigmas, 0.0).astype(jnp.bfloat16)
        grad_vals = jnp.einsum(
            "hqk,qhd->khd", weights, gradout_blk, preferred_element_type=jnp.float32
        )
        grad_weights = jnp.einsum(
            "qhd,khd->hqk", gradout_blk, value_blk, preferred_element_type=jnp.float32
        )
        grad_scores = jnp.where(allowed[None], grad_weights * sigmas * (1.0 - sigmas), 0.0).astype(
            jnp.bfloat16
        )
        grad_qs = (
            jnp.einsum("hqk,khd->qhd", grad_scores, key_blk, preferred_element_type=jnp.float32)
            * score_scale
        )
        grad_ks = (
            jnp.einsum("hqk,qhd->khd", grad_scores, query_blk, preferred_element_type=jnp.float32)
            * score_scale
        )
        return (grad_qs, grad_ks, grad_vals)

    def nothing(unused):
        empty_q = jnp.zeros(query_blk.shape, jnp.float32)
        empty_k = jnp.zeros(key_blk.shape, jnp.float32)
        return (empty_q, empty_k, empty_k)

    return lax.cond(jnp.any(allowed), pair_compute, nothing, 0)


def per_device(
    tokens,
    cotangent,
    block_order,
    sequence_ids,
    attn_gain,
    w_query,
    w_key,
    w_value,
    w_out,
    mlp_gain,
    w_gate,
    w_up,
    w_down,
):
    tok_rows = tokens.shape[0]
    group_rows = tok_rows // 2
    devices = lax.axis_size("seq")
    score_bias = -math.log(tok_rows * devices // 2)
    score_scale = 1.0 / math.sqrt(HD)
    my_index = lax.axis_index("seq")
    boundary = jnp.sum((sequence_ids == 0).astype(jnp.int32))
    my_pos = group_positions(block_order, my_index * tok_rows, tok_rows, group_rows)
    attn_parts = (
        lax.all_gather(w_query.astype(jnp.bfloat16), "seq", axis=0, tiled=True),
        lax.all_gather(w_key.astype(jnp.bfloat16), "seq", axis=0, tiled=True),
        lax.all_gather(w_value.astype(jnp.bfloat16), "seq", axis=0, tiled=True),
        lax.all_gather(w_out.astype(jnp.bfloat16), "seq", axis=1, tiled=True),
        lax.all_gather(attn_gain.astype(jnp.bfloat16), "seq", axis=0, tiled=True),
    )
    query_full, key_full, value_full, out_full = (
        attn_parts[0],
        attn_parts[1],
        attn_parts[2],
        attn_parts[3],
    )
    gain_attn = attn_parts[4].astype(jnp.float32)
    heads_local = query_full.shape[1] // HD
    source = tokens.astype(jnp.float32)
    normed_attn, inverse_attn = normalize(source)
    hidden_attn = (normed_attn * gain_attn).astype(jnp.bfloat16)
    cosine, sine = rope_tables(my_pos, HD)

    def project(weight_full):
        return jnp.dot(hidden_attn, weight_full, preferred_element_type=jnp.float32).reshape(
            tok_rows, heads_local, HD
        )

    queries = rotate(project(query_full), cosine, sine).astype(jnp.bfloat16)
    keys = rotate(project(key_full), cosine, sine).astype(jnp.bfloat16)
    values = project(value_full).astype(jnp.bfloat16)
    key_all = lax.all_gather(keys, "seq", axis=0, tiled=True)
    value_all = lax.all_gather(values, "seq", axis=0, tiled=True)
    piece_rows = key_all.shape[0]
    block_rows = math.gcd(piece_rows, 512)

    def add_block(block_index, partial_value):
        offset = block_index * block_rows
        key_blk = lax.dynamic_slice_in_dim(key_all, offset, block_rows, 0)
        value_blk = lax.dynamic_slice_in_dim(value_all, offset, block_rows, 0)
        key_pos = group_positions(block_order, offset, block_rows, group_rows)
        allowed = visible(my_pos, key_pos, boundary)

        def add_compute(current):
            scores = (
                jnp.einsum("qhd,khd->hqk", queries, key_blk, preferred_element_type=jnp.float32)
                * score_scale
                + score_bias
            )
            weights = jnp.where(allowed[None], jax.nn.sigmoid(scores), 0.0).astype(jnp.bfloat16)
            return current + jnp.einsum(
                "hqk,khd->qhd", weights, value_blk, preferred_element_type=jnp.float32
            )

        def unchanged(current):
            return current

        return lax.cond(jnp.any(allowed), add_compute, unchanged, partial_value)

    attended = lax.fori_loop(
        0, piece_rows // block_rows, add_block, jnp.zeros((tok_rows, heads_local, HD), jnp.float32)
    )
    attended_low = attended.reshape(tok_rows, heads_local * HD).astype(jnp.bfloat16)
    attn_part = jnp.dot(attended_low, out_full, preferred_element_type=jnp.float32)
    residual = source + lax.psum(attn_part, "tp")
    mlp_parts = (
        lax.all_gather(w_gate.astype(jnp.bfloat16), "seq", axis=0, tiled=True),
        lax.all_gather(w_up.astype(jnp.bfloat16), "seq", axis=0, tiled=True),
        lax.all_gather(w_down.astype(jnp.bfloat16), "seq", axis=1, tiled=True),
        lax.all_gather(mlp_gain.astype(jnp.bfloat16), "seq", axis=0, tiled=True),
    )
    gate_full, up_full, down_full = (mlp_parts[0], mlp_parts[1], mlp_parts[2])
    gain_mlp = mlp_parts[3].astype(jnp.float32)
    normed_mlp, inverse_mlp = normalize(residual)
    hidden_mlp = (normed_mlp * gain_mlp).astype(jnp.bfloat16)
    gate = jnp.dot(hidden_mlp, gate_full, preferred_element_type=jnp.float32)
    up_proj = jnp.dot(hidden_mlp, up_full, preferred_element_type=jnp.float32)
    gate_sigma = jax.nn.sigmoid(gate)
    gate_silu = gate * gate_sigma
    activated = (gate_silu * up_proj).astype(jnp.bfloat16)
    mlp_part = jnp.dot(activated, down_full, preferred_element_type=jnp.float32)
    output = (residual + lax.psum(mlp_part, "tp")).astype(jnp.bfloat16)
    grad_w_down = jnp.einsum("tf,td->fd", activated, cotangent, preferred_element_type=jnp.float32)
    grad_act = jnp.einsum("td,fd->tf", cotangent, down_full, preferred_element_type=jnp.float32)
    grad_gate_act = (grad_act * up_proj * gate_sigma * (1.0 + gate * (1.0 - gate_sigma))).astype(
        jnp.bfloat16
    )
    grad_up_act = (grad_act * gate_silu).astype(jnp.bfloat16)
    grad_w_gate = jnp.einsum(
        "td,tf->df", hidden_mlp, grad_gate_act, preferred_element_type=jnp.float32
    )
    grad_w_up = jnp.einsum("td,tf->df", hidden_mlp, grad_up_act, preferred_element_type=jnp.float32)
    hidden_grad_part = jnp.einsum(
        "tf,df->td", grad_gate_act, gate_full, preferred_element_type=jnp.float32
    ) + jnp.einsum("tf,df->td", grad_up_act, up_full, preferred_element_type=jnp.float32)
    grad_hidden_mlp = lax.psum(hidden_grad_part, "tp")
    grad_gain_mlp = jnp.sum(grad_hidden_mlp * normed_mlp, axis=0)
    grad_resid = norm_back(grad_hidden_mlp * gain_mlp, normed_mlp, inverse_mlp) + cotangent.astype(
        jnp.float32
    )
    mlp_shards = (
        lax.psum_scatter(grad_w_gate, "seq", scatter_dimension=0, tiled=True),
        lax.psum_scatter(grad_w_up, "seq", scatter_dimension=0, tiled=True),
        lax.psum_scatter(grad_w_down, "seq", scatter_dimension=1, tiled=True),
        lax.psum_scatter(grad_gain_mlp, "seq", scatter_dimension=0, tiled=True),
    )
    resid_low = grad_resid.astype(jnp.bfloat16)
    grad_w_out = jnp.einsum(
        "tc,td->cd", attended_low, resid_low, preferred_element_type=jnp.float32
    )
    grad_attended = (
        jnp.einsum("td,cd->tc", resid_low, out_full, preferred_element_type=jnp.float32)
        .astype(jnp.bfloat16)
        .reshape(tok_rows, heads_local, HD)
    )
    zero_rows = jnp.zeros((tok_rows, heads_local, HD), jnp.float32)

    def key_turn(turn, carry):
        moving, moving_grads, grad_qsum = carry
        source_index = (my_index + turn) % devices
        key_pos = group_positions(block_order, source_index * tok_rows, tok_rows, group_rows)
        terms = pair_terms(
            queries,
            grad_attended,
            my_pos,
            moving[0],
            moving[1],
            key_pos,
            boundary,
            score_scale,
            score_bias,
        )
        moving_grads = moving_grads + jnp.stack([terms[1], terms[2]])
        moving = from_behind(moving, "seq", -1)
        moving_grads = from_behind(moving_grads, "seq", -1)
        return (moving, moving_grads, grad_qsum + terms[0])

    key_start = (
        jnp.stack([keys, values]),
        jnp.zeros((2, tok_rows, heads_local, HD), jnp.float32),
        zero_rows,
    )
    key_final = lax.fori_loop(0, devices, key_turn, key_start)
    grad_queries = key_final[2]
    grad_keys = key_final[1][0]
    grad_values = key_final[1][1]
    grad_query_lin = (
        unrotate(grad_queries, cosine, sine)
        .reshape(tok_rows, heads_local * HD)
        .astype(jnp.bfloat16)
    )
    grad_key_lin = (
        unrotate(grad_keys, cosine, sine).reshape(tok_rows, heads_local * HD).astype(jnp.bfloat16)
    )
    grad_value_lin = grad_values.reshape(tok_rows, heads_local * HD).astype(jnp.bfloat16)
    grad_w_query = jnp.einsum(
        "td,tc->dc", hidden_attn, grad_query_lin, preferred_element_type=jnp.float32
    )
    grad_w_key = jnp.einsum(
        "td,tc->dc", hidden_attn, grad_key_lin, preferred_element_type=jnp.float32
    )
    grad_w_value = jnp.einsum(
        "td,tc->dc", hidden_attn, grad_value_lin, preferred_element_type=jnp.float32
    )
    attn_grad_part = jnp.einsum(
        "tc,dc->td", grad_query_lin, query_full, preferred_element_type=jnp.float32
    )
    attn_grad_part = attn_grad_part + jnp.einsum(
        "tc,dc->td", grad_key_lin, key_full, preferred_element_type=jnp.float32
    )
    attn_grad_part = attn_grad_part + jnp.einsum(
        "tc,dc->td", grad_value_lin, value_full, preferred_element_type=jnp.float32
    )
    grad_hidden_attn = lax.psum(attn_grad_part.astype(jnp.bfloat16), "tp").astype(jnp.float32)
    grad_gain_attn = jnp.sum(grad_hidden_attn * normed_attn, axis=0)
    grad_tokens = norm_back(grad_hidden_attn * gain_attn, normed_attn, inverse_attn) + grad_resid
    attn_shards = (
        lax.psum_scatter(grad_w_query, "seq", scatter_dimension=0, tiled=True),
        lax.psum_scatter(grad_w_key, "seq", scatter_dimension=0, tiled=True),
        lax.psum_scatter(grad_w_value, "seq", scatter_dimension=0, tiled=True),
        lax.psum_scatter(grad_w_out, "seq", scatter_dimension=1, tiled=True),
        lax.psum_scatter(grad_gain_attn, "seq", scatter_dimension=0, tiled=True),
    )
    return (
        output,
        grad_tokens,
        attn_shards[4],
        attn_shards[0],
        attn_shards[1],
        attn_shards[2],
        attn_shards[3],
        mlp_shards[3],
        mlp_shards[0],
        mlp_shards[1],
        mlp_shards[2],
    )


def solution(mesh):
    in_specs = (
        P("seq", None),
        P("seq", None),
        P(),
        P(),
        P("seq"),
        P("seq", "tp"),
        P("seq", "tp"),
        P("seq", "tp"),
        P("tp", "seq"),
        P("seq"),
        P("seq", "tp"),
        P("seq", "tp"),
        P("tp", "seq"),
    )
    out_specs = (
        P("seq", None),
        P("seq", None),
        P("seq"),
        P("seq", "tp"),
        P("seq", "tp"),
        P("seq", "tp"),
        P("tp", "seq"),
        P("seq"),
        P("seq", "tp"),
        P("seq", "tp"),
        P("tp", "seq"),
    )
    return jax.shard_map(
        per_device, mesh=mesh, in_specs=in_specs, out_specs=out_specs, check_vma=False
    )
```

profile of v0, /device:TPU:0, one launch (start us, length us, event | category | flops | bytes accessed | tf_op | source)
XLA Modules:
  0.0 4762.1 jit_solution(10720290702147216940)
XLA Ops:
  13.5 42.3 all-gather
  58.0 32.1 all-gather.16.cloned.1.call-done
  94.3 73.9 %all-gather.12.cloned.1.call-done = bf16[2048,1024]{1,0:T(8,128)(2,1)} async-done(((bf16[128,1024]{1,0:T(8,128)(2,1)}), bf16[2048,1024]{1,0:T(8,128)(2,1)}) %all-gather.12.cloned.1.call-update) | async-done | bytes 4194320 | tf_op jit(solution)/shard_map/all_gather | solution.py:154
  173.2 73.1 %all-gather.18.cloned.1.call-done = bf16[2048,1024]{1,0:T(8,128)(2,1)} async-done(((bf16[128,1024]{1,0:T(8,128)(2,1)}), bf16[2048,1024]{1,0:T(8,128)(2,1)}) %all-gather.18.cloned.1.call-update) | async-done | bytes 4194320 | tf_op jit(solution)/shard_map/all_gather | solution.py:155
  251.8 85.5 %all-gather.14.cloned.1.call-done = bf16[2048,8,128]{0,2,1:T(8,128)(2,1)} async-done(((bf16[128,8,128]{0,2,1:T(8,128)(2,1)}), bf16[2048,8,128]{0,2,1:T(8,128)(2,1)}) %all-gather.14.cloned.1.call-update) | async-done | bytes 4194320 | tf_op jit(solution)/shard_map/all_gather | solution.py:180
  343.8 71.4 %all-gather.20.cloned.1.call-done = bf16[2048,8,128]{2,0,1:T(8,128)(2,1)} async-done(((bf16[128,8,128]{2,0,1:T(8,128)(2,1)}), bf16[2048,8,128]{2,0,1:T(8,128)(2,1)}) %all-gather.20.cloned.1.call-update) | async-done | bytes 4194320 | tf_op jit(solution)/shard_map/all_gather | solution.py:181
  415.2 20.1 while.39
  435.5 70.5 %all-gather.22.cloned.1.call-done = bf16[1024,2048]{1,0:T(8,128)(2,1)} async-done(((bf16[1024,128]{1,0:T(8,128)(2,1)}), bf16[1024,2048]{1,0:T(8,128)(2,1)}) %all-gather.22.cloned.1.call-update) | async-done | bytes 4194320 | tf_op jit(solution)/shard_map/all_gather | solution.py:156
  518.5 38.1 all-gather.1
  558.2 166.2 %all-gather.24.cloned.1.call-done = bf16[2048,4096]{1,0:T(8,128)(2,1)} async-done(((bf16[128,4096]{1,0:T(8,128)(2,1)}), bf16[2048,4096]{1,0:T(8,128)(2,1)}) %all-gather.24.cloned.1.call-update) | async-done | bytes 16777232 | tf_op jit(solution)/shard_map/all_gather | solution.py:215
  724.4 9.4 fusion.76
  733.8 184.1 %all-gather.26.cloned.1.call-done = bf16[2048,4096]{1,0:T(8,128)(2,1)} async-done(((bf16[128,4096]{1,0:T(8,128)(2,1)}), bf16[2048,4096]{1,0:T(8,128)(2,1)}) %all-gather.26.cloned.1.call-update) | async-done | bytes 16777232 | tf_op jit(solution)/shard_map/all_gather | solution.py:216
  918.0 9.4 fusion.77
  927.4 241.9 %all-gather.28.cloned.1.call-done = bf16[4096,2048]{1,0:T(8,128)(2,1)} async-done(((bf16[4096,128]{1,0:T(8,128)(2,1)}), bf16[4096,2048]{1,0:T(8,128)(2,1)}) %all-gather.28.cloned.1.call-update) | async-done | bytes 16777232 | tf_op jit(solution)/shard_map/all_gather | solution.py:217
  1169.3 14.4 multiply_convert_fusion
  1183.7 9.5 fusion.78
  1193.2 13.0 fusion.79
  1206.2 12.6 convolution_add_fusion.2
  1221.3 17.1 all-reduce.12.cloned.1.call-done
  1245.7 670.1 %while.40 = (s32[]{:T(128)}, bf16[2,128,8,128]{3,1,2,0:T(8,128)(2,1)}, f32[2,128,8,128]{3,1,2,0:T(8,128)}, f32[128,8,128]{2,0,1:T(8,128)}, s32[]{:T(128)}, /*ind...) while((s32[]{:T(128)}, ...), condition=%wide.region_19.20_spmd.clone, body=%wide.region_14.19_spmd.clone.sunk | while | flops 170344336 | bytes 23123052 | solution.py:291
  1260.5 32.9 collective-permute-done
  1310.5 31.6 collective-permute-done
  1359.2 30.7 collective-permute-done
  1406.9 29.7 collective-permute-done
  1451.4 28.8 collective-permute-done
  1497.3 27.9 collective-permute-done
  1539.9 27.0 collective-permute-done
  1584.0 25.9 collective-permute-done
  1627.0 24.9 collective-permute-done
  1669.0 23.9 collective-permute-done
  1710.0 22.9 collective-permute-done
  1749.9 21.8 collective-permute-done
  1786.5 20.8 collective-permute-done
  1813.9 8.5 collective-permute-start.1
  1824.4 19.8 collective-permute-done
  1861.3 18.7 collective-permute-done
  1897.1 17.7 collective-permute-done
  1948.4 13.5 fusion.81
  1963.1 13.2 fusion.82
  1977.7 13.4 fusion.83
  1994.5 78.8 %all-reduce.2 = (f32[2048]{0:T(1024)S(1)}, f32[2048]{0:T(1024)S(1)}) all-reduce(f32[2048]{0:T(1024)S(1)} %get-tuple-element.721, f32[2048]{0:T(1024)S(1)} %get-tuple-element.719), channel_id=2, replica_groups=mesh['seq'=16,'tp'=2] {'seq'}, use_global_device_ids=true, to_apply=%region_23.24.clone | all-reduce | flops 4096 | bytes 32768
  2076.8 55.9 %reduce-scatter.8.cloned.1.call-done = f32[128,1024]{1,0:T(8,128)} async-done(((f32[2048,1024]{1,0:T(8,128)}), f32[128,1024]{1,0:T(8,128)}) %reduce-scatter.8.cloned.1.call-update) | async-done | bytes 524304 | tf_op jit(solution)/shard_map/reduce_scatter | solution.py:326
  2132.8 183.1 %reduce-scatter.10.cloned.1.call-done = f32[128,1024]{1,0:T(8,128)} async-done(((f32[2048,1024]{1,0:T(8,128)}), f32[128,1024]{1,0:T(8,128)}) %reduce-scatter.10.cloned.1.call-update) | async-done | bytes 524304 | tf_op jit(solution)/shard_map/reduce_scatter | solution.py:327
  2315.9 183.1 %reduce-scatter.12.cloned.1.call-done = f32[128,1024]{1,0:T(8,128)} async-done(((f32[2048,1024]{1,0:T(8,128)}), f32[128,1024]{1,0:T(8,128)}) %reduce-scatter.12.cloned.1.call-update) | async-done | bytes 524304 | tf_op jit(solution)/shard_map/reduce_scatter | solution.py:328
  2499.0 183.1 %reduce-scatter.14.cloned.1.call-done = f32[1024,128]{1,0:T(8,128)} async-done(((f32[1024,2048]{1,0:T(8,128)}), f32[1024,128]{1,0:T(8,128)}) %reduce-scatter.14.cloned.1.call-update) | async-done | bytes 524304 | tf_op jit(solution)/shard_map/reduce_scatter | solution.py:329
  2682.1 688.8 %reduce-scatter.16.cloned.1.call-done = f32[128,4096]{1,0:T(8,128)} async-done(((f32[2048,4096]{1,0:T(8,128)}), f32[128,4096]{1,0:T(8,128)}) %reduce-scatter.16.cloned.1.call-update) | async-done | bytes 2097168 | tf_op jit(solution)/shard_map/reduce_scatter | solution.py:250
  3370.9 692.0 %reduce-scatter.18.cloned.1.call-done = f32[128,4096]{1,0:T(8,128)} async-done(((f32[2048,4096]{1,0:T(8,128)}), f32[128,4096]{1,0:T(8,128)}) %reduce-scatter.18.cloned.1.call-update) | async-done | bytes 2097168 | tf_op jit(solution)/shard_map/reduce_scatter | solution.py:251
  4062.9 692.2 %reduce-scatter.20.cloned.1.call-done = f32[4096,128]{1,0:T(8,128)} async-done(((f32[4096,2048]{1,0:T(8,128)}), f32[4096,128]{1,0:T(8,128)}) %reduce-scatter.20.cloned.1.call-update) | async-done | bytes 2097168 | tf_op jit(solution)/shard_map/reduce_scatter | solution.py:252
  (441 shorter events, 374.8 us)
Async XLA Ops:
  7.2 83.0 %all-gather.16.cloned.1.call-start = ((), (), s32[]{:S(2)}) async-start(), calls=%async_computation.9 | async-start | bytes 4456448 | tf_op jit(solution)/shard_map/all_gather | solution.py:153
  9.0 159.2 %all-gather.12.cloned.1.call-start = ((), (), s32[]{:S(2)}) async-start(), calls=%async_computation.7 | async-start | bytes 4456448 | tf_op jit(solution)/shard_map/all_gather | solution.py:154
  10.9 235.4 %all-gather.18.cloned.1.call-start = ((), (), s32[]{:S(2)}) async-start(), calls=%async_computation.10 | async-start | bytes 4456448 | tf_op jit(solution)/shard_map/all_gather | solution.py:155
  12.8 324.5 %all-gather.14.cloned.1.call-start = ((), (), s32[]{:S(2)}) async-start(), calls=%async_computation.8 | async-start | bytes 4456448 | tf_op jit(solution)/shard_map/all_gather | solution.py:180
  173.2 242.0 %all-gather.20.cloned.1.call-start = ((), (), s32[]{:S(2)}) async-start(), calls=%async_computation.11 | async-start | bytes 4456448 | tf_op jit(solution)/shard_map/all_gather | solution.py:181
  250.0 255.9 %all-gather.22.cloned.1.call-start = ((), (), s32[]{:S(2)}) async-start(), calls=%async_computation.12 | async-start | bytes 4456448 | tf_op jit(solution)/shard_map/all_gather | solution.py:156
  250.9 305.7 %all-reduce.8.cloned.1.call-start = ((), (), s32[]{:S(2)}) async-start(), calls=%async_computation.13 | async-start | bytes 2097152 | tf_op jit(solution)/shard_map/psum | solution.py:213
  509.9 214.5 %all-gather.24.cloned.1.call-start = ((), (), s32[]{:S(2)}) async-start(), calls=%async_computation.14 | async-start | bytes 17825792 | tf_op jit(solution)/shard_map/all_gather | solution.py:215
  512.7 405.3 %all-gather.26.cloned.1.call-start = ((), (), s32[]{:S(2)}) async-start(), calls=%async_computation.15 | async-start | bytes 17825792 | tf_op jit(solution)/shard_map/all_gather | solution.py:216
  515.6 653.7 %all-gather.28.cloned.1.call-start = ((), (), s32[]{:S(2)}) async-start(), calls=%async_computation.16 | async-start | bytes 17825792 | tf_op jit(solution)/shard_map/all_gather | solution.py:217
  518.4 720.0 %all-reduce.12.cloned.1.call-start = ((), (), s32[]{:S(2)}) async-start(), calls=%async_computation.25 | async-start | bytes 4194304 | tf_op jit(solution)/shard_map/psum | solution.py:230
  1218.8 774.2 %all-reduce.10.cloned.1.call-start = ((), (), s32[]{:S(2)}) async-start(), calls=%async_computation.17 | async-start | bytes 1048576 | tf_op jit(solution)/shard_map/psum | solution.py:322
  1253.7 39.7 collective-permute-start.1
  1259.1 34.3 collective-permute-start
  1300.0 42.1 collective-permute-start.1
  1308.6 33.5 collective-permute-start
  1348.7 41.1 collective-permute-start.1
  1357.2 32.6 collective-permute-start
  1396.4 40.2 collective-permute-start.1
  1405.0 31.7 collective-permute-start
  1443.3 36.9 collective-permute-start.1
  1449.5 30.7 collective-permute-start
  1486.8 38.4 collective-permute-start.1
  1495.4 29.8 collective-permute-start
  1534.2 32.7 collective-permute-start.1
  1538.0 28.9 collective-permute-start
  1573.5 36.4 collective-permute-start.1
  1582.0 27.9 collective-permute-start
  1616.5 35.4 collective-permute-start.1
  1625.1 26.8 collective-permute-start
  1658.5 34.4 collective-permute-start.1
  1667.1 25.8 collective-permute-start
  1699.5 33.3 collective-permute-start.1
  1708.1 24.8 collective-permute-start
  1739.5 32.3 collective-permute-start.1
  1748.0 23.8 collective-permute-start
  1778.4 28.9 collective-permute-start.1
  1784.6 22.7 collective-permute-start
  1813.9 30.2 collective-permute-start.1
  1850.8 29.2 collective-permute-start.1
  1889.0 25.8 collective-permute-start.1
  1927.3 205.5 %reduce-scatter.8.cloned.1.call-start = ((), (), s32[]{:S(2)}) async-start(), calls=%async_computation.18 | async-start | bytes 8912896 | tf_op jit(solution)/shard_map/reduce_scatter | solution.py:326
  1932.1 383.8 %reduce-scatter.10.cloned.1.call-start = ((), (), s32[]{:S(2)}) async-start(), calls=%async_computation.19 | async-start | bytes 8912896 | tf_op jit(solution)/shard_map/reduce_scatter | solution.py:327
  1936.7 562.3 %reduce-scatter.12.cloned.1.call-start = ((), (), s32[]{:S(2)}) async-start(), calls=%async_computation.20 | async-start | bytes 8912896 | tf_op jit(solution)/shard_map/reduce_scatter | solution.py:328
  1941.5 740.6 %reduce-scatter.14.cloned.1.call-start = ((), (), s32[]{:S(2)}) async-start(), calls=%async_computation.21 | async-start | bytes 8912896 | tf_op jit(solution)/shard_map/reduce_scatter | solution.py:329
  1947.2 1423.7 %reduce-scatter.16.cloned.1.call-start = ((), (), s32[]{:S(2)}) async-start(), calls=%async_computation.22 | async-start | bytes 35651584 | tf_op jit(solution)/shard_map/reduce_scatter | solution.py:250
  1961.9 2101.0 %reduce-scatter.18.cloned.1.call-start = ((), (), s32[]{:S(2)}) async-start(), calls=%async_computation.23 | async-start | bytes 35651584 | tf_op jit(solution)/shard_map/reduce_scatter | solution.py:251
  1976.3 2778.7 %reduce-scatter.20.cloned.1.call-start = ((), (), s32[]{:S(2)}) async-start(), calls=%async_computation.24 | async-start | bytes 35651584 | tf_op jit(solution)/shard_map/reduce_scatter | solution.py:252
  (44 other events, 925.6 us)
Sparse Core Ops, SparseCore 0:
  11.4 78.7 all-gather.15
  93.5 74.6 all-gather.11
  171.6 74.6 all-gather.17
  249.4 87.7 all-gather.13
  340.4 74.6 all-gather.19
  418.3 87.6 all-gather.21
  510.0 17.7 all-reduce.7
  531.6 192.8 all-gather.23
  728.1 189.7 all-gather.25
  921.5 247.8 all-gather.27
  1218.9 19.4 all-reduce.11
  1927.4 20.6 all-reduce.9
  1951.1 181.6 reduce-scatter.7
  2135.6 180.2 reduce-scatter.9
  2318.7 180.2 reduce-scatter.11
  2501.8 180.2 reduce-scatter.13
  2685.0 685.8 reduce-scatter.15
  3373.8 689.0 reduce-scatter.17
  4066.0 689.0 reduce-scatter.19
where the time goes:
time: 4780 us; the launch traced here: 4760 us
  waiting for transfers between devices  4100 us (86%)
  matrix products  167 us (3%)
  blocking collectives  159 us (3%)
  other arithmetic  129 us (3%)
  starting transfers between devices  124 us (3%)
  local copies, waits for them, and re-layouts  54 us (1%)
    reduce_scatter x1, waiting for transfers between devices, per_device(): lax.psum_scatter(grad_w_down, 'seq', scatter_dimension=1, tiled=True)  692 us
    reduce_scatter x1, waiting for transfers between devices, per_device(): lax.psum_scatter(grad_w_up, 'seq', scatter_dimension=0, tiled=True)  692 us
    reduce_scatter x1, waiting for transfers between devices, per_device(): lax.psum_scatter(grad_w_gate, 'seq', scatter_dimension=0, tiled=True)  689 us
    ppermute x32, waiting for transfers between devices, from_behind(): lax.ppermute(value, axis, [(i, (i + by) % length) for i in range(length)])  405 us
    all_gather x1, waiting for transfers between devices, per_device(): lax.all_gather(w_down.astype(jnp.bfloat16), 'seq', axis=1, tiled=True)  242 us
    all_gather x1, waiting for transfers between devices, per_device(): lax.all_gather(w_up.astype(jnp.bfloat16), 'seq', axis=0, tiled=True)  184 us
    reduce_scatter x1, waiting for transfers between devices, per_device(): lax.psum_scatter(grad_w_out, 'seq', scatter_dimension=1, tiled=True)  183 us
    reduce_scatter x1, waiting for transfers between devices, per_device(): lax.psum_scatter(grad_w_key, 'seq', scatter_dimension=0, tiled=True)  183 us
  transfers between devices with their start and end apart: 51, of which 33 were waited for; matrix products, arithmetic and copies ran while one was open for 4% of the time, Pallas kernels for 0%

commit v1 on v0

--- a/solution.py
+++ b/solution.py
@@ -1,8 +1,11 @@
+import functools
 import math
 
 import jax
 import jax.numpy as jnp
 from jax import lax
+from jax.experimental import pallas as pl
+from jax.experimental.pallas import tpu as pltpu
 from jax.sharding import PartitionSpec as P
 
 HD = 128
@@ -126,7 +129,7 @@
     return lax.cond(jnp.any(allowed), pair_compute, nothing, 0)
 
 
-def per_device(
+def per_device_gathered(
     tokens,
     cotangent,
     block_order,
@@ -344,6 +347,501 @@
     )
 
 
+MESH = pl.DeviceIdType.MESH
+ANY = pl.BlockSpec(memory_space=pl.ANY)
+VMEM = pl.BlockSpec(memory_space=pltpu.VMEM)
+
+
+def place():
+    seq = lax.axis_index("seq")
+    return (seq // 4, (seq // 2) % 2, seq % 2, lax.axis_index("tp"))
+
+
+def device(z, y, x, core):
+    return (z * 4 + y * 2 + x, core)
+
+
+def meet(peers):
+    barrier = pltpu.get_barrier_semaphore()
+    for peer in peers:
+        pl.semaphore_signal(barrier, inc=1, device_id=peer, device_id_type=MESH)
+    pl.semaphore_wait(barrier, len(peers))
+
+
+def push(source, target, send_sem, recv_sem, peer):
+    copy = pltpu.make_async_remote_copy(
+        src_ref=source,
+        dst_ref=target,
+        send_sem=send_sem,
+        recv_sem=recv_sem,
+        device_id=peer,
+        device_id_type=MESH,
+    )
+    copy.start()
+    return copy
+
+
+def plane_peers():
+    z, y, x, core = place()
+    return [device((z + d) % 4, y, x, core) for d in (1, 2, 3)] + [
+        device(z, 1 - y, x, core),
+        device(z, y, x, 1 - core),
+    ]
+
+
+def gather_kernel(mine, out, send, recv, local):
+    z, y, x, core = place()
+    rows = mine.shape[0]
+    meet(plane_peers())
+
+    def slot(zz, yy, cc):
+        return out.at[pl.ds(pl.multiple_of((zz * 4 + yy * 2 + cc) * rows, rows), rows)]
+
+    keep = pltpu.make_async_copy(mine, slot(z, y, core), local)
+    keep.start()
+    sent = []
+
+    def go(index, source, target, peer):
+        copy = push(source, target, send.at[index], recv.at[index], peer)
+        sent.append(copy)
+        return copy
+
+    along_z, along_y, across = {}, {}, {}
+    for d in (1, 3, 2):
+        along_z[d] = go(d - 1, mine, slot(z, y, core), device((z + d) % 4, y, x, core))
+    along_y[0] = go(3, mine, slot(z, y, core), device(z, 1 - y, x, core))
+    across[0] = go(7, mine, slot(z, y, core), device(z, y, x, 1 - core))
+    for d in (1, 3, 2):
+        along_z[d].wait_recv()
+        part = slot((z - d) % 4, y, core)
+        along_y[d] = go(3 + d, part, part, device(z, 1 - y, x, core))
+        across[d] = go(7 + d, part, part, device(z, y, x, 1 - core))
+    for d in (0, 1, 3, 2):
+        along_y[d].wait_recv()
+        part = slot((z - d) % 4, 1 - y, core)
+        across[4 + d] = go(11 + d, part, part, device(z, y, x, 1 - core))
+    for d in range(8):
+        across[d].wait_recv()
+    for copy in sent:
+        copy.wait_send()
+    keep.wait()
+
+
+def gather_plane(mine):
+    rows, width = mine.shape
+    return pl.pallas_call(
+        gather_kernel,
+        out_shape=jax.ShapeDtypeStruct((rows * 16, width), mine.dtype),
+        in_specs=[ANY],
+        out_specs=ANY,
+        scratch_shapes=[
+            pltpu.SemaphoreType.DMA((15,)),
+            pltpu.SemaphoreType.DMA((15,)),
+            pltpu.SemaphoreType.DMA,
+        ],
+        compiler_params=pltpu.CompilerParams(collective_id=0, has_side_effects=True),
+    )(mine)
+
+
+def reduce_kernel(part, out, pair, half, ybuf, zsum, zbuf, send, recv):
+    z, y, x, core = place()
+    rows = out.shape[0]
+    meet(plane_peers())
+
+    def span(zz, yy, cc):
+        return pl.ds(pl.multiple_of((zz * 4 + yy * 2 + cc) * rows, rows), rows)
+
+    order = [(d, other) for other in (1, 0) for d in (2, 1, 3, 0)]
+    across, along_y, along_z = {}, {}, {}
+    for i, (d, other) in enumerate(order):
+        zz, yy = (z + d) % 4, (y + other) % 2
+        across[i] = push(
+            part.at[span(zz, yy, 1 - core)],
+            pair.at[i],
+            send.at[i],
+            recv.at[i],
+            device(z, y, x, 1 - core),
+        )
+    f32 = jnp.float32
+    for i, (d, other) in enumerate(order):
+        zz, yy = (z + d) % 4, (y + other) % 2
+        across[i].wait_recv()
+        total = part[span(zz, yy, core)].astype(f32) + pair[i].astype(f32)
+        half[i] = total.astype(half.dtype)
+        if other:
+            along_y[i] = push(
+                half.at[i], ybuf.at[i], send.at[8 + i], recv.at[8 + i], device(z, 1 - y, x, core)
+            )
+    for i, (d, other) in enumerate(order[4:]):
+        along_y[i].wait_recv()
+        if d:
+            total = half[4 + i].astype(f32) + ybuf[i].astype(f32)
+            zsum[i] = total.astype(zsum.dtype)
+            along_z[i] = push(
+                zsum.at[i],
+                zbuf.at[i],
+                send.at[12 + i],
+                recv.at[12 + i],
+                device((z + d) % 4, y, x, core),
+            )
+    for i in range(3):
+        along_z[i].wait_recv()
+    out[...] = (half[7].astype(f32) + ybuf[3].astype(f32)) + (
+        zbuf[0].astype(f32) + zbuf[1].astype(f32) + zbuf[2].astype(f32)
+    )
+    for copies in (across, along_y, along_z):
+        for copy in copies.values():
+            copy.wait_send()
+
+
+def reduce_plane(part):
+    rows, width = part.shape[0] // 16, part.shape[1]
+
+    def room(count):
+        return pltpu.VMEM((count, rows, width), part.dtype)
+
+    return pl.pallas_call(
+        reduce_kernel,
+        out_shape=jax.ShapeDtypeStruct((rows, width), jnp.float32),
+        in_specs=[VMEM],
+        out_specs=VMEM,
+        scratch_shapes=[
+            room(8),
+            room(8),
+            room(4),
+            room(3),
+            room(3),
+            pltpu.SemaphoreType.DMA((15,)),
+            pltpu.SemaphoreType.DMA((15,)),
+        ],
+        compiler_params=pltpu.CompilerParams(collective_id=1, has_side_effects=True),
+    )(part)
+
+
+def weights_kernel(*refs):
+    z, y, x, core = place()
+    mine = z * 2 + y
+    count = (len(refs) - 5) // 2
+    groups, outs = refs[:count], refs[count : 2 * count]
+    send, recv, xsend, xrecv, local = refs[2 * count :]
+    mate = device(z, y, 1 - x, core)
+    meet([device((z + d // 2) % 4, (y + d) % 2, x, core) for d in range(1, 8)] + [mate])
+
+    def slot(group, zz, yy, xx):
+        owner = (zz * 2 + yy) * 2 + xx
+        out = outs[group]
+        if group % 2 == 0:
+            rows = groups[group].shape[1]
+            return out.at[pl.ds(pl.multiple_of(owner * rows, rows), rows)]
+        columns = groups[group].shape[2]
+        return out.at[:, pl.ds(pl.multiple_of(owner * columns, columns), columns)]
+
+    keeps, spread, passed = [], {}, []
+    for group in range(count):
+        keep = pltpu.make_async_copy(
+            groups[group].at[mine], slot(group, z, y, x), local.at[group]
+        )
+        keep.start()
+        keeps.append(keep)
+        passed.append(
+            push(
+                groups[group].at[mine],
+                slot(group, z, y, x),
+                xsend.at[group, 0],
+                xrecv.at[group, 0],
+                mate,
+            )
+        )
+        for d in (4, 5, 2, 3, 6, 7, 1):
+            zz, yy = (z + d // 2) % 4, (y + d) % 2
+            spread[group, d] = push(
+                groups[group].at[zz * 2 + yy],
+                slot(group, z, y, x),
+                send.at[group, d],
+                recv.at[group, d],
+                device(zz, yy, x, core),
+            )
+    for group in range(count):
+        for d in (1, 2, 3, 6, 7, 4, 5):
+            spread[group, d].wait_recv()
+            part = slot(group, (z - d // 2) % 4, (y + d) % 2, x)
+            passed.append(push(part, part, xsend.at[group, d], xrecv.at[group, d], mate))
+    for copy in passed:
+        copy.wait_recv()
+    for copy in passed:
+        copy.wait_send()
+    for copy in spread.values():
+        copy.wait_send()
+    for keep in keeps:
+        keep.wait()
+
+
+def spread_weights(groups):
+    shapes = []
+    for index, group in enumerate(groups):
+        _, rows, columns = group.shape
+        whole = (rows * 16, columns) if index % 2 == 0 else (rows, columns * 16)
+        shapes.append(jax.ShapeDtypeStruct(whole, group.dtype))
+    count = len(groups)
+    return pl.pallas_call(
+        weights_kernel,
+        out_shape=shapes,
+        in_specs=[ANY] * count,
+        out_specs=[ANY] * count,
+        scratch_shapes=[pltpu.SemaphoreType.DMA((count, 8))] * 4
+        + [pltpu.SemaphoreType.DMA((count,))],
+        compiler_params=pltpu.CompilerParams(collective_id=2, has_side_effects=True),
+    )(*groups)
+
+
+def swap_kernel(mine, other, send, recv, *, across):
+    z, y, x, core = place()
+    peer = device(z, y, x, 1 - core) if across else device(z, y, 1 - x, core)
+    meet([peer])
+    push(mine, other, send, recv, peer).wait()
+
+
+def swap(mine, across, ident):
+    return pl.pallas_call(
+        functools.partial(swap_kernel, across=across),
+        out_shape=jax.ShapeDtypeStruct(mine.shape, mine.dtype),
+        in_specs=[ANY],
+        out_specs=ANY,
+        scratch_shapes=[pltpu.SemaphoreType.DMA] * 2,
+        compiler_params=pltpu.CompilerParams(
+            collective_id=ident, has_side_effects=True
+        ),
+    )(mine)
+
+
+def return_kernel(*refs):
+    z, y, x, core = place()
+    mine = z * 2 + y
+    count = (len(refs) - 3) // 2
+    groups, outs = refs[:count], refs[count : 2 * count]
+    send, recv, local = refs[2 * count :]
+    meet([device((z + d // 2) % 4, (y + d) % 2, x, core) for d in range(1, 8)])
+    copies, keeps = [], []
+    for group in range(count):
+        keep = pltpu.make_async_copy(
+            groups[group].at[mine], outs[group].at[mine], local.at[group]
+        )
+        keep.start()
+        keeps.append(keep)
+        for d in (4, 5, 2, 3, 6, 7, 1):
+            zz, yy = (z + d // 2) % 4, (y + d) % 2
+            copies.append(
+                push(
+                    groups[group].at[zz * 2 + yy],
+                    outs[group].at[mine],
+                    send.at[group, d],
+                    recv.at[group, d],
+                    device(zz, yy, x, core),
+                )
+            )
+    for copy in copies:
+        copy.wait_recv()
+    for copy in copies:
+        copy.wait_send()
+    for keep in keeps:
+        keep.wait()
+
+
+def return_grads(groups):
+    count = len(groups)
+    return pl.pallas_call(
+        return_kernel,
+        out_shape=[jax.ShapeDtypeStruct(group.shape, group.dtype) for group in groups],
+        in_specs=[ANY] * count,
+        out_specs=[ANY] * count,
+        scratch_shapes=[pltpu.SemaphoreType.DMA((count, 8))] * 2
+        + [pltpu.SemaphoreType.DMA((count,))],
+        compiler_params=pltpu.CompilerParams(collective_id=5, has_side_effects=True),
+    )(*groups)
+
+
+def plane_positions(block_order, x, tok_rows, group_rows):
+    rows = jnp.arange(tok_rows * 8, dtype=jnp.int32)
+    stored = (rows // tok_rows) * (2 * tok_rows) + x * tok_rows + rows % tok_rows
+    slots = jnp.arange(block_order.shape[0], dtype=jnp.int32)
+    onehot = ((stored // group_rows)[:, None] == slots[None, :]).astype(jnp.int32)
+    return jnp.sum(onehot * block_order[None, :], axis=1) * group_rows + stored % group_rows
+
+
+def turn(values, cosine, sine):
+    half_dim = values.shape[-1] // 2
+    first, second = values[..., :half_dim], values[..., half_dim:]
+    return jnp.concatenate(
+        [first * cosine - second * sine, second * cosine + first * sine], axis=-1
+    )
+
+
+def per_device_split(
+    tokens,
+    cotangent,
+    block_order,
+    sequence_ids,
+    attn_gain,
+    w_query,
+    w_key,
+    w_value,
+    w_out,
+    mlp_gain,
+    w_gate,
+    w_up,
+    w_down,
+):
+    bf16, f32 = jnp.bfloat16, jnp.float32
+    tok_rows, width = tokens.shape
+    own = tok_rows // 2
+    score_bias = -math.log(tok_rows * 16 // 2)
+    score_scale = 1.0 / math.sqrt(HD)
+    z, y, x, core = place()
+    boundary = jnp.sum((sequence_ids == 0).astype(jnp.int32))
+    my_pos = plane_positions(block_order, x, tok_rows, own)
+    key_pos = jnp.concatenate([my_pos, plane_positions(block_order, 1 - x, tok_rows, own)])
+    my_start = jnp.where(my_pos >= boundary, boundary, 0)
+    allowed = (key_pos[None, :] <= my_pos[:, None]) & (key_pos[None, :] >= my_start[:, None])
+
+    def by_columns(weight):
+        rows, columns = weight.shape
+        return weight.astype(bf16).reshape(rows, 8, columns // 8).transpose(1, 0, 2)
+
+    def by_rows(weight):
+        rows, columns = weight.shape
+        return weight.astype(bf16).reshape(8, rows // 8, columns)
+
+    groups = (
+        jnp.concatenate([by_columns(w_query), by_columns(w_key), by_columns(w_value)], axis=2),
+        by_rows(w_out),
+        jnp.concatenate([by_columns(w_gate), by_columns(w_up)], axis=2),
+        by_rows(w_down),
+    )
+    head_in, head_out, hidden_in, hidden_out = spread_weights(groups)
+    gains = lax.all_gather(jnp.stack([attn_gain, mlp_gain]), "seq", axis=1, tiled=True)
+    gains = gains.astype(bf16).astype(f32)
+    gain_attn, gain_mlp = gains[0], gains[1]
+    tokens_own = lax.dynamic_slice_in_dim(tokens, core * own, own, 0)
+    cot_own = lax.dynamic_slice_in_dim(cotangent, core * own, own, 0)
+    source = gather_plane(tokens_own).astype(f32)
+    cot = gather_plane(cot_own)
+    normed_attn, _ = normalize(source)
+    hidden_attn = (normed_attn * gain_attn).astype(bf16)
+    cosine, sine = rope_tables(my_pos, HD)
+    qkv = jnp.dot(hidden_attn, head_in, preferred_element_type=f32)
+    query = turn(qkv[:, :HD], cosine, sine).astype(bf16)
+    key = turn(qkv[:, HD : 2 * HD], cosine, sine).astype(bf16)
+    key_value = jnp.concatenate([key, qkv[:, 2 * HD :].astype(bf16)], axis=1)
+    key_value = jnp.concatenate([key_value, swap(key_value, False, 3)], axis=0)
+    keys, values = key_value[:, :HD], key_value[:, HD:]
+    scores = jnp.dot(query, keys.T, preferred_element_type=f32) * score_scale + score_bias
+    sigmas = jax.nn.sigmoid(scores)
+    weights = jnp.where(allowed, sigmas, 0.0).astype(bf16)
+    attended = jnp.dot(weights, values, preferred_element_type=f32).astype(bf16)
+    attn_part = jnp.dot(attended, head_out, preferred_element_type=f32).astype(bf16)
+    residual = tokens_own.astype(f32) + reduce_plane(attn_part)
+    normed_mlp, inverse_mlp = normalize(residual)
+    hidden_mlp = gather_plane((normed_mlp * gain_mlp).astype(bf16))
+    gate_up = jnp.dot(hidden_mlp, hidden_in, preferred_element_type=f32)
+    units = gate_up.shape[1] // 2
+    gate, up_proj = gate_up[:, :units], gate_up[:, units:]
+    gate_sigma = jax.nn.sigmoid(gate)
+    gate_silu = gate * gate_sigma
+    activated = (gate_silu * up_proj).astype(bf16)
+    grad_act = jnp.dot(cot, hidden_out.T, preferred_element_type=f32)
+    grad_gate_act = (grad_act * up_proj * gate_sigma * (1.0 + gate * (1.0 - gate_sigma))).astype(
+        bf16
+    )
+    grad_pair = jnp.concatenate([grad_gate_act, (grad_act * gate_silu).astype(bf16)], axis=1)
+    hidden_grad_part = jnp.dot(grad_pair, hidden_in.T, preferred_element_type=f32).astype(bf16)
+    grad_hidden_mlp = reduce_plane(hidden_grad_part)
+    mlp_part = jnp.dot(activated, hidden_out, preferred_element_type=f32).astype(bf16)
+    output_own = (residual + reduce_plane(mlp_part)).astype(bf16)
+    grad_gain_mlp = jnp.sum(grad_hidden_mlp * normed_mlp, axis=0)
+    grad_resid = norm_back(grad_hidden_mlp * gain_mlp, normed_mlp, inverse_mlp) + cot_own.astype(
+        f32
+    )
+    resid_low = gather_plane(grad_resid.astype(bf16))
+    grad_head_out = jnp.dot(attended.T, resid_low, preferred_element_type=f32)
+    grad_attended = jnp.dot(resid_low, head_out.T, preferred_element_type=f32).astype(bf16)
+    grad_values = jnp.dot(weights.T, grad_attended, preferred_element_type=f32)
+    grad_weights = jnp.dot(grad_attended, values.T, preferred_element_type=f32)
+    grad_scores = jnp.where(allowed, grad_weights * sigmas * (1.0 - sigmas), 0.0).astype(bf16)
+    grad_query = jnp.dot(grad_scores, keys, preferred_element_type=f32) * score_scale
+    grad_keys = jnp.dot(grad_scores.T, query, preferred_element_type=f32) * score_scale
+    grad_kv = jnp.concatenate([grad_keys, grad_values], axis=1)
+    plane_rows = tok_rows * 8
+    grad_kv = grad_kv[:plane_rows] + swap(grad_kv[plane_rows:].astype(bf16), False, 3).astype(f32)
+    grad_lin = jnp.concatenate(
+        [
+            turn(grad_query, cosine, -sine).astype(bf16),
+            turn(grad_kv[:, :HD], cosine, -sine).astype(bf16),
+            grad_kv[:, HD:].astype(bf16),
+        ],
+        axis=1,
+    )
+    attn_grad_part = jnp.dot(grad_lin, head_in.T, preferred_element_type=f32).astype(bf16)
+    grad_hidden_attn = reduce_plane(attn_grad_part)
+    normed_own, inverse_own = normalize(tokens_own.astype(f32))
+    grad_gain_attn = jnp.sum(grad_hidden_attn * normed_own, axis=0)
+    grad_tokens_own = norm_back(grad_hidden_attn * gain_attn, normed_own, inverse_own) + grad_resid
+
+    def whole_rows(mine, ident):
+        other = swap(mine, True, ident)
+        first = jnp.where(core == 0, mine, other)
+        second = jnp.where(core == 0, other, mine)
+        return jnp.concatenate([first, second], axis=0)
+
+    grad_head_in = jnp.dot(hidden_attn.T, grad_lin, preferred_element_type=f32)
+    grad_hidden_in = jnp.dot(hidden_mlp.T, grad_pair, preferred_element_type=f32)
+    grad_hidden_out = jnp.dot(activated.T, cot, preferred_element_type=f32)
+
+    def rows_of(grad):
+        return grad.reshape(8, 2, grad.shape[0] // 16, grad.shape[1]).transpose(1, 0, 2, 3)
+
+    def columns_of(grad):
+        split = grad.reshape(grad.shape[0], 8, 2, grad.shape[1] // 16)
+        return split.transpose(2, 1, 0, 3)
+
+    def joined(split, ident):
+        mine = lax.dynamic_index_in_dim(split, x, 0, keepdims=False)
+        other = lax.dynamic_index_in_dim(split, 1 - x, 0, keepdims=False).astype(bf16)
+        return (mine + swap(other, False, ident).astype(f32)).astype(bf16)
+
+    returned = return_grads(
+        (
+            joined(jnp.concatenate([rows_of(grad_head_in), rows_of(grad_hidden_in)], axis=3), 8),
+            joined(
+                jnp.concatenate([columns_of(grad_head_out), columns_of(grad_hidden_out)], axis=2), 9
+            ),
+        )
+    )
+    into, outof = returned[0].astype(f32), returned[1].astype(f32)
+
+    def columns_back(first, count):
+        piece = into[:, :, first : first + count].transpose(1, 0, 2)
+        return piece.reshape(piece.shape[0], 8 * count)
+
+    def rows_back(first, count):
+        return outof[:, first : first + count].reshape(8 * count, outof.shape[2])
+
+    gain_sums = lax.psum(jnp.stack([grad_gain_attn, grad_gain_mlp]), ("seq", "tp"))
+    mine = lax.dynamic_slice_in_dim(gain_sums, lax.axis_index("seq") * tok_rows, tok_rows, 1)
+    return (
+        whole_rows(output_own, 6),
+        whole_rows(grad_tokens_own, 7),
+        mine[0],
+        columns_back(0, HD),
+        columns_back(HD, HD),
+        columns_back(2 * HD, HD),
+        rows_back(0, HD),
+        mine[1],
+        columns_back(3 * HD, units),
+        columns_back(3 * HD + units, units),
+        rows_back(HD, units),
+    )
+
+
 def solution(mesh):
     in_specs = (
         P("seq", None),
@@ -373,6 +871,7 @@
         P("seq", "tp"),
         P("tp", "seq"),
     )
+    fits = mesh.shape["seq"] == 16 and mesh.shape["tp"] == 2
     return jax.shard_map(
-        per_device, mesh=mesh, in_specs=in_specs, out_specs=out_specs, check_vma=False
-    )
+        per_device_split if fits else per_device_gathered, mesh=mesh, in_specs=in_specs, out_specs=out_specs, check_vma=False
+    )

time: 4780 us -> 917 us (0.19)
  waiting for transfers between devices: 4100 us -> 0 us
  Pallas kernels: 0 us -> 643 us
  starting transfers between devices: 124 us -> 0 us
  matrix products: 167 us -> 78.2 us
  other arithmetic: 129 us -> 50.8 us
  blocking collectives: 159 us -> 81.1 us
    reduce_scatter x7 -> x0, waiting for transfers between devices: 2680 us -> none  [the longest x1 692 us: per_device(): lax.psum_scatter(grad_w_down, 'seq', scatter_dimension=1, tiled=True)]
    all_gather x9 -> x0, waiting for transfers between devices: 999 us -> none  [the longest x1 242 us: per_device(): lax.all_gather(w_down.astype(jnp.bfloat16), 'seq', axis=1, tiled=True)]
    pallas_call x0 -> x16, Pallas kernels: none -> 643 us  [the longest x4 176 us: reduce_plane(): pl.pallas_call(reduce_kernel, out_shape=jax.ShapeDtypeStruct((rows, width...]
    ppermute x32 -> x0, waiting for transfers between devices: 405 us -> none  [from_behind(): lax.ppermute(value, axis, [(i, (i + by) % length) for i in range(length)])]
    ppermute x32 -> x0, starting transfers between devices: 123 us -> none  [from_behind(): lax.ppermute(value, axis, [(i, (i + by) % length) for i in range(length)])]
    dot_general x37 -> x18, matrix products: 158 us -> 78.2 us  [the longest x1 8.32 us: per_device_split(): gate_up = jnp.dot(hidden_mlp, hidden_in, preferred_element_type=f32)]
    unnamed x1 -> x0, blocking collectives: 78.8 us -> none
    add x34 -> x3, other arithmetic: 71.4 us -> 3.98 us  [the longest x1 2.77 us: per_device_split(): norm_back(grad_hidden_attn * gain_attn, normed_own, inverse_own)]
  transfers between devices with their start and end apart: 51 -> 0, of which waited for: 33 -> 0; matrix products, arithmetic and copies ran while one was open for 4% -> 0% of each run, Pallas kernels for 0% -> 0%
where the time goes in v1:
time: 917 us; the launch traced here: 903 us
  Pallas kernels  643 us (70%)
  blocking collectives  81.1 us (9%)
  matrix products  78.2 us (9%)
  other arithmetic  50.8 us (6%)
  local copies, waits for them, and re-layouts  48.1 us (5%)
    pallas_call x4, Pallas kernels, reduce_plane(): pl.pallas_call(reduce_kernel, out_shape=jax.ShapeDtypeStruct((rows, width...  176 us
    pallas_call x4, Pallas kernels, gather_plane(): pl.pallas_call(gather_kernel, out_shape=jax.ShapeDtypeStruct((rows * 16,...  136 us
    pallas_call x6, Pallas kernels, swap(): pl.pallas_call(functools.partial(swap_kernel, across=across), out_shape=j...  129 us
    pallas_call x1, Pallas kernels, spread_weights(): pl.pallas_call(weights_kernel, out_shape=shapes, in_specs=[ANY] * count,...  113 us
    pallas_call x1, Pallas kernels, return_grads(): pl.pallas_call(return_kernel, out_shape=[jax.ShapeDtypeStruct(group.shape...  89.5 us
    all_gather x1, blocking collectives, per_device_split(): lax.all_gather(jnp.stack([attn_gain, mlp_gain]), 'seq', axis=1, tiled=True)  42.2 us
    psum x1, blocking collectives, per_device_split(): lax.psum(jnp.stack([grad_gain_attn, grad_gain_mlp]), ('seq', 'tp'))  38.9 us
    unnamed x72, local copies, waits for them, and re-layouts  18.8 us

profile of v1, /device:TPU:0, one launch (start us, length us, event | category | flops | bytes accessed | tf_op | source)
XLA Modules:
  0.0 903.1 jit_solution(619228593629643156)
XLA Ops:
  2.9 42.2 %all_gather.3 = bf16[2,2048]{1,0:T(2,128)(2,1)S(1)} all-gather(bf16[2,128]{1,0:T(2,128)(2,1)S(1)} %pad_maximum_fusion.14), channel_id=1, replica_groups=mesh['seq'=16,'tp'=2] {'seq'}, dimensions={1}, use_global_device_ids=true | all-gather | bytes 8704 | tf_op jit(solution)/shard_map/all_gather | solution.py:721
  51.4 1.9 pad_maximum_fusion.7.refs_0_
  64.8 25.4 %shard_map.219 = bf16[1024,2048]{1,0:T(8,128)(2,1)} custom-call(bf16[64,2048]{1,0:T(8,128)(2,1)} %constant_dynamic-slice_fusion.1.mine), custom_call_target="tpu_custom_call" | custom-call | tf_op jit(solution)/shard_map/pallas_call | solution.py:432
  90.2 40.5 %shard_map.212 = bf16[1024,2048]{1,0:T(8,128)(2,1)} custom-call(bf16[64,2048]{1,0:T(8,128)(2,1)} %get-tuple-element.63.mine), custom_call_target="tpu_custom_call" | custom-call | tf_op jit(solution)/shard_map/pallas_call | solution.py:432
  130.7 3.1 fusion
  133.8 112.7 %shard_map.213 = (bf16[2048,384]{1,0:T(8,128)(2,1)}, bf16[128,2048]{1,0:T(8,128)(2,1)}, bf16[2048,1024]{1,0:T(8,128)(2,1)}, bf16[512,2048]{1,0:T(8,128)(2,1)}) custom-call(bf16[8,128,384]{2,1,0:T(8,128)(2,1)} %pad_maximum_fusion.7.refs_0_, bf16[8,128,128]{2,1,0:T(8,128)(2,1)} %bitcast.116, bf16[8,128,1024]{2,1,0:T(8,128)(2,1)} %pad_maximum_fusion.refs_2_, ...), custom_call_target="tpu_custom_call" | custom-call | tf_op jit(solution)/shard_map/pallas_call | solution.py:586
  246.6 5.1 fusion.21
  251.7 2.5 fusion.60
  255.2 13.8 %shard_map.214 = bf16[1024,256]{1,0:T(8,128)(2,1)} custom-call(bf16[1024,256]{1,0:T(8,128)(2,1)} %pad_maximum_fusion.8.mine), custom_call_target="tpu_custom_call" | custom-call | tf_op jit(solution)/shard_map/pallas_call | solution.py:605
  270.4 5.7 select_convert_fusion.1
  278.1 3.2 convolution_convert_fusion.2.part
  281.3 60.8 %shard_map.215 = f32[64,2048]{1,0:T(8,128)} custom-call(bf16[1024,2048]{1,0:T(8,128)(2,1)} %convolution_convert_fusion.2.part), custom_call_target="tpu_custom_call" | custom-call | tf_op jit(solution)/shard_map/pallas_call | solution.py:503
  344.3 34.8 %shard_map.216 = bf16[1024,2048]{1,0:T(8,128)(2,1)} custom-call(bf16[64,2048]{1,0:T(8,128)(2,1)} %multiply_convert_fusion.3.mine), custom_call_target="tpu_custom_call" | custom-call | tf_op jit(solution)/shard_map/pallas_call | solution.py:432
  379.1 8.3 fusion.95
  387.5 4.0 multiply_convert_fusion.1
  392.8 6.2 convolution_convert_fusion.3.part
  399.0 39.0 %shard_map.220 = f32[64,2048]{1,0:T(8,128)} custom-call(bf16[1024,2048]{1,0:T(8,128)(2,1)} %convolution_convert_fusion.3.part), custom_call_target="tpu_custom_call" | custom-call | tf_op jit(solution)/shard_map/pallas_call | solution.py:503
  438.1 6.9 fusion.98
  445.0 5.6 copy.124
  451.7 6.3 convolution_convert_fusion.1.part
  458.0 38.6 %shard_map.217 = f32[64,2048]{1,0:T(8,128)} custom-call(bf16[1024,2048]{1,0:T(8,128)(2,1)} %convolution_convert_fusion.1.part), custom_call_target="tpu_custom_call" | custom-call | tf_op jit(solution)/shard_map/pallas_call | solution.py:503
  496.6 6.7 fusion.17
  503.2 4.1 copy.143
  507.3 35.6 %shard_map.221 = bf16[1024,2048]{1,0:T(8,128)(2,1)} custom-call(bf16[64,2048]{1,0:T(8,128)(2,1)} %fusion.92.mine), custom_call_target="tpu_custom_call" | custom-call | tf_op jit(solution)/shard_map/pallas_call | solution.py:432
  543.0 3.4 convolution_convert_fusion.4
  546.4 5.2 select_convert_fusion
  555.6 2.0 convolution_multiply_fusion.1
  561.3 14.6 %shard_map.222 = bf16[1024,256]{1,0:T(8,128)(2,1)} custom-call(bf16[1024,256]{1,0:T(8,128)(2,1)} %fusion.25.mine), custom_call_target="tpu_custom_call" | custom-call | tf_op jit(solution)/shard_map/pallas_call | solution.py:605
  577.2 2.6 fusion.58
  580.6 5.1 fusion.19
  585.9 1.9 copy-done
  589.4 30.6 %shard_map.226 = bf16[8,640,128]{2,1,0:T(8,128)(2,1)} custom-call(bf16[8,640,128]{2,1,0:T(8,128)(2,1)} %fusion.18.mine), custom_call_target="tpu_custom_call" | custom-call | tf_op jit(solution)/shard_map/pallas_call | solution.py:605
  620.0 3.6 fusion.15.refs_1_
  623.6 4.3 convolution_convert_fusion.part
  628.0 37.5 %shard_map.223 = f32[64,2048]{1,0:T(8,128)} custom-call(bf16[1024,2048]{1,0:T(8,128)(2,1)} %convolution_convert_fusion.part), custom_call_target="tpu_custom_call" | custom-call | tf_op jit(solution)/shard_map/pallas_call | solution.py:503
  666.8 38.9 %psum.7 = f32[2,2048]{1,0:T(2,128)S(1)} all-reduce(f32[2,2048]{1,0:T(2,128)S(1)} %pad_maximum_fusion.13), channel_id=1, replica_groups=mesh['seq'=16,'tp'=2] {'seq','tp'}, use_global_device_ids=true, to_apply=%region_10.11 | all-reduce | flops 4096 | bytes 32768 | tf_op jit(solution)/shard_map/psum | solution.py:828
  706.2 2.8 fusion.49
  709.0 1.9 shard_map.218
  712.8 2.3 shard_map.224
  717.4 4.2 fusion.9.mine
  721.6 65.4 %shard_map.225 = bf16[8,128,1408]{2,1,0:T(8,128)(2,1)} custom-call(bf16[8,128,1408]{2,1,0:T(8,128)(2,1)} %fusion.9.mine), custom_call_target="tpu_custom_call" | custom-call | tf_op jit(solution)/shard_map/pallas_call | solution.py:605
  787.0 5.4 fusion.8.refs_0_
  792.4 89.5 %shard_map.227 = (bf16[8,128,1408]{2,1,0:T(8,128)(2,1)}, bf16[8,640,128]{2,1,0:T(8,128)(2,1)}) custom-call(bf16[8,128,1408]{2,1,0:T(8,128)(2,1)} %fusion.8.refs_0_, bf16[8,640,128]{2,1,0:T(8,128)(2,1)} %fusion.15.refs_1_), custom_call_target="tpu_custom_call" | custom-call | tf_op jit(solution)/shard_map/pallas_call | solution.py:652
  881.9 1.9 slice.141
  883.8 2.7 slice.144
  887.9 2.6 slice_bitcast_fusion
  890.5 1.9 copy.129
  898.8 1.9 copy.128
  (127 shorter events, 56.0 us)
Async XLA Ops:
  0.6 54.5 %copy-start.13 = (bf16[128,2048]{1,0:T(8,128)(2,1)S(1)}, bf16[128,2048]{1,0:T(8,128)(2,1)}, u32[]{:S(2)}) copy-start(bf16[128,2048]{1,0:T(8,128)(2,1)} %param.14) | copy-start | bytes 1572868
  0.7 57.0 %copy-start.10 = (f32[128,4096]{1,0:T(8,128)S(1)}, f32[128,4096]{1,0:T(8,128)}, u32[]{:S(2)}) copy-start(f32[128,4096]{1,0:T(8,128)} %param.23) | copy-start | bytes 6291460
  61.4 2.4 copy-start.11
  254.2 21.9 %copy-start.17 = (bf16[1024,64]{1,0:T(8,128)(2,1)}, bf16[1024,64]{1,0:T(8,128)(2,1)S(1)}, u32[]{:S(2)}) copy-start(bf16[1024,64]{1,0:T(8,128)(2,1)S(1)} %get-tuple-element.76) | copy-start | bytes 393220
  254.2 21.9 %copy-start.19 = (bf16[1024,64]{1,0:T(8,128)(2,1)}, bf16[1024,64]{1,0:T(8,128)(2,1)S(1)}, u32[]{:S(2)}) copy-start(bf16[1024,64]{1,0:T(8,128)(2,1)S(1)} %get-tuple-element.79) | copy-start | bytes 393220
  270.4 276.1 %copy-start.15 = (bf16[2048,256]{1,0:T(8,128)(2,1)}, bf16[2048,256]{1,0:T(8,128)(2,1)S(1)}, u32[]{:S(2)}) copy-start(bf16[2048,256]{1,0:T(8,128)(2,1)S(1)} %pad_maximum_fusion.5) | copy-start | bytes 3145732
  276.1 2.0 copy-start.6
  276.1 2.0 copy-start.23
  281.3 60.9 %copy-start.5 = (bf16[64,2048]{1,0:T(8,128)(2,1)S(1)}, bf16[64,2048]{1,0:T(8,128)(2,1)}, u32[]{:S(2)}) copy-start(bf16[64,2048]{1,0:T(8,128)(2,1)} %get-tuple-element.63.mine) | copy-start | bytes 786436
  343.4 107.4 %copy-start.2 = (f32[64,2048]{1,0:T(8,128)}, f32[64,2048]{1,0:T(8,128)S(1)}, u32[]{:S(2)}) copy-start(f32[64,2048]{1,0:T(8,128)S(1)} %get-tuple-element.65) | copy-start | bytes 1572868
  379.1 8.4 copy-start.8
  379.1 8.4 copy-start.26
  387.5 5.4 copy-start.25
  391.5 1.0 copy-start.28
  391.5 1.3 copy-start.30
  445.0 5.6 copy-start.4
  445.0 5.9 copy-start.14
  458.0 38.6 %copy-start.29 = (bf16[1024,512]{0,1:T(8,128)(2,1)S(1)}, bf16[1024,512]{0,1:T(8,128)(2,1)}, u32[]{:S(2)}) copy-start(bf16[1024,512]{0,1:T(8,128)(2,1)} %copy-done.28) | copy-start | bytes 3145732
  507.3 35.7 %copy-start.24 = (bf16[128,2048]{1,0:T(8,128)(2,1)S(1)}, bf16[128,2048]{1,0:T(8,128)(2,1)}, u32[]{:S(2)}) copy-start(bf16[128,2048]{1,0:T(8,128)(2,1)} %get-tuple-element.18) | copy-start | bytes 1572868
  546.4 5.2 copy-start.7
  551.6 2.2 copy-start.1
  553.8 1.8 copy-start.16
  555.6 2.1 copy-start.18
  555.6 2.1 copy-start.20
  575.9 1.3 copy-start.12
  580.6 5.1 copy-start.21
  585.7 2.2 copy-start
  585.7 2.5 copy-start.3
  620.0 3.6 copy-start.22
  620.0 3.6 copy-start.27
  881.8 4.6 copy-start.9
